TPU v7x, 512 devices: a whole 4x8x8 slice. The times are simulated.
512 devices in a mesh: blk: 32 (over y, x), harm: 16 (over z, core).
Axes of the slice: x: 4, y: 8, z: 8, core: 2. Of those that a mesh axis runs over, the one named last changes fastest.
Arguments:
- samples: float32 [16384, 128], P(('blk', 'harm')), may hold values from -6 to 6
- store: float32 [2, 48, 16384, 128], P(None, 'harm', 'blk'), may hold values from -0.6 to 0.6
- phase: float32 [5], replicated, may hold values from -3.140625 to 3.140625
- patch_row: int32 [16384], P('blk'), may hold values from 0 to 4
- harm_counts: int32 [5], replicated, may hold values from 8 to 48
- freq_index: int32 [5, 48], replicated, may hold values from 1 to 63
- blade_counts: int32 [5], replicated, may hold values from 20 to 80
Outputs:
- new_store: float32 [2, 48, 16384, 128], P(None, 'harm', 'blk')
- lower_lagged: float32 [16384, 128], P(('blk', 'harm'))
- upper_lagged: float32 [16384, 128], P(('blk', 'harm'))
All inputs are finite; a program needn't handle non-finite values.
Results may differ from a plain program's by a relative error of at most 0.00002.
Values sent between devices are 32-bit elements; how exact they have to be, the bound alone decides.
A program may use at most 64 MiB of HBM per device.

v0:
```python
import jax
import jax.numpy as jnp
from jax import lax
from jax.sharding import PartitionSpec as P

relax_rate = 0.3


def from_behind(block, axis, distance):
    devices = range(lax.axis_size(axis))
    route = [((i - distance) % len(devices), i) for i in devices]
    return lax.ppermute(block, axis, route)


def shards(samples, store, phase, patch_row, harm_counts, freq_index, blade_counts):
    gathered = lax.all_gather(samples, "harm", axis=0, tiled=True)
    slot_count = store.shape[1]
    row_count = freq_index.shape[0]
    first_slot = lax.axis_index("harm") * slot_count
    frequency = lax.dynamic_slice_in_dim(freq_index, first_slot, slot_count, 1).astype(jnp.float32)
    slot_ids = first_slot + jnp.arange(slot_count, dtype=jnp.int32)
    active_row = (slot_ids[None, :] < harm_counts[:, None]).astype(jnp.float32)
    angle_row = frequency * phase[:, None]
    lag_row = 2.0 * jnp.pi * frequency / blade_counts.astype(jnp.float32)[:, None]
    onehot = patch_row[:, None] == jnp.arange(row_count, dtype=jnp.int32)[None, :]

    def per_patch(table):
        return jnp.sum(jnp.where(onehot[None, :, :], table.T[:, None, :], 0.0), axis=2)

    angle_now = per_patch(angle_row)[:, :, None]
    angle_lag = per_patch(lag_row)[:, :, None]
    active_mask = per_patch(active_row)[:, :, None] > 0.5
    sample_col = gathered[None, :, :]
    cos_old = store[0]
    sin_old = store[1]
    cos_new = jnp.where(
        active_mask,
        cos_old + relax_rate * (2.0 * sample_col * jnp.cos(angle_now) - cos_old),
        cos_old,
    )
    sin_new = jnp.where(
        active_mask,
        sin_old + relax_rate * (2.0 * sample_col * jnp.sin(angle_now) - sin_old),
        sin_old,
    )
    back_angle = angle_now - angle_lag
    ahead_angle = angle_now + angle_lag
    back_part = jnp.sum(
        jnp.where(active_mask, cos_new * jnp.cos(back_angle) + sin_new * jnp.sin(back_angle), 0.0),
        axis=0,
    )
    ahead_part = jnp.sum(
        jnp.where(
            active_mask, cos_new * jnp.cos(ahead_angle) + sin_new * jnp.sin(ahead_angle), 0.0
        ),
        axis=0,
    )
    new_store = jnp.stack([cos_new, sin_new])
    summed = lax.psum_scatter(
        jnp.stack([back_part, ahead_part]), "harm", scatter_dimension=1, tiled=True
    )
    lower_lagged = from_behind(summed[0], "blk", 1)
    upper_lagged = from_behind(summed[1], "blk", -1)
    return (new_store, lower_lagged, upper_lagged)


def solution(mesh):
    in_specs = (
        P(("blk", "harm"), None),
        P(None, "harm", "blk", None),
        P(),
        P("blk"),
        P(),
        P(),
        P(),
    )
    out_specs = (P(None, "harm", "blk", None), P(("blk", "harm"), None), P(("blk", "harm"), None))
    return jax.shard_map(shards, mesh=mesh, in_specs=in_specs, out_specs=out_specs, check_vma=False)
```

profile of v0, /device:TPU:1, one launch (start us, length us, event | category | flops | bytes accessed | tf_op | source)
XLA Modules:
  0.0 118.1 jit_solution(8640709716201541647)
XLA Ops:
  7.2 0.0 reduce-scatter.2.cloned.1.call-start
  7.2 0.7 convert_element_type.16
  7.9 0.7 iota_compare_fusion
  8.6 0.7 compare_convert_fusion
  9.3 0.8 multiply_bitcast_fusion
  10.1 0.1 select_reduce_fusion.2
  10.2 25.4 %all_gather.3 = f32[512,128]{1,0:T(8,128)S(1)} all-gather(f32[32,128]{1,0:T(8,128)} %param.7), channel_id=1, replica_groups=mesh['blk'=32,'harm'=16] {'harm'}, dimensions={0}, use_global_device_ids=true | all-gather | bytes 278528 | tf_op jit(solution)/shard_map/all_gather | solution.py:16
  35.6 0.2 add_cosine_fusion
  35.8 0.0 copy-start
  35.9 3.6 %select_reduce_fusion.1 = (f32[512,128]{1,0:T(8,128)S(1)}, f32[512,128]{1,0:T(8,128)S(1)}) fusion(f32[2,3,512,128]{3,2,1,0:T(8,128)} %param.8, f32[3,512]{1,0:T(4,128)S(1)} %get-tuple-element.13, f32[3,512]{1,0:T(4,128)S(1)} %get-tuple-element.16, f32[3,512]{1,0:T(4,128)S(1)} %get-tuple-element.15, f32[3,512]{1,0:T(4,128)S(1)} %get-tuple-element.17, ...), kind=kLoop, calls=%fused_computation.10 | loop fusion | flops 3801088 | bytes 2397696 | tf_op jit(solution)/shard_map/reduce_sum | solution.py:48
  39.4 0.8 pad_maximum_fusion.1
  40.2 0.0 reduce-scatter.2.cloned.1.call-update
  40.3 0.0 copy-done
  40.3 0.8 add_select_fusion.3
  41.1 54.0 %reduce-scatter.2.cloned.1.call-done = f32[2,32,128]{2,1,0:T(8,128)} async-done(((f32[2,512,128]{2,1,0:T(8,128)}), f32[2,32,128]{2,1,0:T(8,128)}) %reduce-scatter.2.cloned.1.call-update) | async-done | bytes 32784 | tf_op jit(solution)/shard_map/reduce_scatter | solution.py:59
  95.1 0.7 slice_bitcast_fusion
  95.9 6.4 %collective-permute-start.1 = (f32[32,128]{1,0:T(8,128)S(1)}, f32[32,128]{1,0:T(8,128)S(1)}, u32[]{:S(2)}, u32[]{:S(2)}) collective-permute-start(f32[32,128]{1,0:T(8,128)S(1)} %get-tuple-element.10), channel_id=1, source_target_pairs={{16,0},{32,16},{48,32},{64,48},{80,64},{96,80},{112,96},{128,112},... | collective-permute-start | bytes 49160 | tf_op jit(solution)/shard_map/ppermute | solution.py:12
  102.2 1.9 %collective-permute-start = (f32[32,128]{1,0:T(8,128)S(1)}, f32[32,128]{1,0:T(8,128)S(1)}, u32[]{:S(2)}, u32[]{:S(2)}) collective-permute-start(f32[32,128]{1,0:T(8,128)S(1)} %get-tuple-element.11), channel_id=1, source_target_pairs={{496,0},{0,16},{16,32},{32,48},{48,64},{64,80},{80,96},{96,112},{1... | collective-permute-start | bytes 49160 | tf_op jit(solution)/shard_map/ppermute | solution.py:12
  104.2 1.2 %pad_maximum_fusion = f32[2,3,512,128]{3,2,1,0:T(8,128)} fusion(f32[1,3,512,128]{3,2,1,0:T(8,128)S(1)} %get-tuple-element.9, f32[1,3,512,128]{3,2,1,0:T(8,128)S(1)} %get-tuple-element.8), kind=kLoop, calls=%fused_computation | loop fusion | flops 393216 | bytes 3145728 | tf_op jit(solution)/shard_map/stack | solution.py:58
  105.4 0.0 collective-permute-done.1
  105.4 4.6 %collective-permute-done = f32[32,128]{1,0:T(8,128)S(1)} collective-permute-done((f32[32,128]{1,0:T(8,128)S(1)}, f32[32,128]{1,0:T(8,128)S(1)}, u32[]{:S(2)}, u32[]{:S(2)}) %collective-permute-start) | collective-permute-done | bytes 16416 | tf_op jit(solution)/shard_map/ppermute | solution.py:12
  110.1 0.6 copy.14
  110.7 0.6 copy.15
  (3 shorter events, 0.0 us)
Async XLA Ops:
  7.2 88.0 %reduce-scatter.2.cloned.1.call-start = ((), (), s32[]{:S(2)}) async-start(), calls=%async_computation.1 | async-start | bytes 557056 | tf_op jit(solution)/shard_map/reduce_scatter | solution.py:59
  35.8 4.4 %copy-start = (f32[2,3,512,128]{3,2,1,0:T(8,128)S(1)}, f32[2,3,512,128]{3,2,1,0:T(8,128)}, u32[]{:S(2)}) copy-start(f32[2,3,512,128]{3,2,1,0:T(8,128)} %param.8) | copy-start | bytes 4718596
  95.9 9.6 %collective-permute-start.1 = (f32[32,128]{1,0:T(8,128)S(1)}, f32[32,128]{1,0:T(8,128)S(1)}, u32[]{:S(2)}, u32[]{:S(2)}) collective-permute-start(f32[32,128]{1,0:T(8,128)S(1)} %get-tuple-element.10), channel_id=1, source_target_pairs={{16,0},{32,16},{48,32},{64,48},{80,64},{96,80},{112,96},{128,112},... | collective-permute-start | bytes 49160 | tf_op jit(solution)/shard_map/ppermute | solution.py:12
  102.2 7.8 %collective-permute-start = (f32[32,128]{1,0:T(8,128)S(1)}, f32[32,128]{1,0:T(8,128)S(1)}, u32[]{:S(2)}, u32[]{:S(2)}) collective-permute-start(f32[32,128]{1,0:T(8,128)S(1)} %get-tuple-element.11), channel_id=1, source_target_pairs={{496,0},{0,16},{16,32},{32,48},{48,64},{64,80},{80,96},{96,112},{1... | collective-permute-start | bytes 49160 | tf_op jit(solution)/shard_map/ppermute | solution.py:12
Sparse Core Ops, SparseCore 0:
  40.4 54.6 reduce-scatter.1
where the time goes:
time: 119 us; the launch traced here: 118 us
  waiting for transfers between devices  58.7 us (49%)
  blocking collectives  25.4 us (21%)
  between operations  14.1 us (12%)
  other arithmetic  9.56 us (8%)
  starting transfers between devices  8.34 us (7%)
  local copies, waits for them, and re-layouts  1.95 us (2%)
    reduce_scatter x1, waiting for transfers between devices, shards(): lax.psum_scatter(jnp.stack([back_part, ahead_part]), 'harm', scatter_dime...  54 us
    all_gather x1, blocking collectives, shards(): gathered = lax.all_gather(samples, 'harm', axis=0, tiled=True)  25.4 us
    ppermute x2, starting transfers between devices, from_behind(): return lax.ppermute(block, axis, route)  8.3 us
    ppermute x2, waiting for transfers between devices, from_behind(): return lax.ppermute(block, axis, route)  4.63 us
    reduce_sum x1, other arithmetic, shards(): jnp.sum(jnp.where(active_mask, cos_new * jnp.cos(back_angle) + sin_new *...  3.56 us
  transfers between devices with their start and end apart: 3, of which 2 were waited for; matrix products, arithmetic and copies ran while one was open for 2% of the time, Pallas kernels for 0%

commit v1 on v0

v1 whole, which is shorter than its diff:
```python
import functools

import jax
import jax.numpy as jnp
from jax import lax
from jax.experimental import pallas as pl
from jax.experimental.pallas import tpu as pltpu
from jax.sharding import PartitionSpec as P

MESH = pl.DeviceIdType.MESH
relax_rate = 0.3
LANES = 128
SUB = 8


def distances(ring):
    far = [ring // 2]
    for d in range(ring // 2 - 1, 0, -1):
        far += [d, ring - d]
    return far + [0]


def fourier_kernel(
    n_blk,
    n_harm,
    samples_hbm,
    store_hbm,
    phase,
    patch_row,
    harm_counts,
    freq_index,
    blade_counts,
    new_store,
    lower,
    upper,
    store,
    gathered,
    freq,
    rows,
    coef,
    mine,
    theirs,
    inbox,
    outbox,
    arrived,
    load_sem,
    pair_send,
    pair_recv,
    sum_send,
    sum_recv,
    ring_send,
    ring_recv,
    fwd_send,
    fwd_recv,
):
    slots, patches = store.shape[1], store.shape[2]
    row_count, slot_total = freq_index.shape
    ring = n_harm // 2
    share = patches // n_harm
    tiles = share // SUB
    blk = lax.axis_index("blk")
    harm = lax.axis_index("harm")
    chip, core = harm // 2, harm % 2
    partner = 2 * chip + 1 - core
    after = lax.rem(blk + 1, n_blk)
    before = lax.rem(blk + n_blk - 1, n_blk)
    hops = distances(ring)

    def peer(d):
        return 2 * lax.rem(chip + d, ring) + core

    barrier = pltpu.get_barrier_semaphore()
    pl.semaphore_signal(barrier, 1, device_id=(blk, partner), device_id_type=MESH)
    for d in hops:
        if d:
            pl.semaphore_signal(barrier, 1, device_id=(blk, peer(d)), device_id_type=MESH)
        for b in (after, before):
            pl.semaphore_signal(barrier, 1, device_id=(b, peer(d)), device_id_type=MESH)

    own = pltpu.make_async_copy(samples_hbm, gathered.at[harm], load_sem.at[2 * slots])
    own.start()
    loads = []
    for part in range(2):
        for j in range(slots):
            load = pltpu.make_async_copy(
                store_hbm.at[part, j], store.at[part, j], load_sem.at[part * slots + j]
            )
            load.start()
            loads.append(load)

    sub = lax.broadcasted_iota(jnp.int32, (SUB, LANES), 0)
    lane = lax.broadcasted_iota(jnp.int32, (SUB, LANES), 1)
    freq[...] = jnp.zeros((SUB, LANES), jnp.float32)
    freq[:row_count, :slot_total] = freq_index[...].astype(jnp.float32)
    frequency = freq[...]

    def by_row(ref, other):
        out = jnp.full((SUB, LANES), other)
        for r in range(row_count):
            out = jnp.where(sub == r, ref[r], out)
        return out

    now = frequency * by_row(phase, jnp.float32(0))
    blades = by_row(blade_counts, jnp.int32(1)).astype(jnp.float32)
    lag = 2.0 * jnp.pi * frequency / blades
    active = lane < by_row(harm_counts, jnp.int32(0))
    now_cos, now_sin = jnp.cos(now), jnp.sin(now)
    back, ahead = now - lag, now + lag
    back_cos, back_sin = jnp.cos(back), jnp.sin(back)
    ahead_cos, ahead_sin = jnp.cos(ahead), jnp.sin(ahead)
    gain = 2.0 * relax_rate
    keep = 1.0 - relax_rate
    zero = jnp.zeros((SUB, LANES), jnp.float32)

    def spread(table):
        return jnp.broadcast_to(jnp.sum(table, axis=1, keepdims=True), (SUB, LANES))

    for j in range(slots):
        here = lane == harm * slots + j
        on = active & here
        for i, table in enumerate((back_cos, back_sin, ahead_cos, ahead_sin)):
            coef[j, i] = spread(jnp.where(on, keep * table, zero))
        coef[j, 4] = spread(jnp.where(on, gain * now_cos, zero))
        coef[j, 5] = spread(jnp.where(on, gain * now_sin, zero))
        coef[j, 6] = spread(jnp.where(here, jnp.where(active, keep, 1.0), zero))
    back_gain = spread(jnp.where(active, gain * (now_cos * back_cos + now_sin * back_sin), zero))
    ahead_gain = spread(jnp.where(active, gain * (now_cos * ahead_cos + now_sin * ahead_sin), zero))

    for i in range(patches // LANES):
        line = jnp.broadcast_to(patch_row[i : i + 1, :], (LANES, LANES))
        rows[pl.ds(i * LANES, LANES), :] = line.T

    def pick(table, row):
        return jnp.take_along_axis(table, row, axis=0, mode="promise_in_bounds")

    for load in loads:
        load.wait()
    own.wait()

    tables = [[coef[j, i] for i in range(4)] for j in range(slots)]

    def partial(base):
        row = rows[pl.ds(base, SUB), :]
        back_sum, ahead_sum = zero, zero
        for j in range(slots):
            c, s = store[0, j, pl.ds(base, SUB), :], store[1, j, pl.ds(base, SUB), :]
            back_sum += pick(tables[j][0], row) * c + pick(tables[j][1], row) * s
            ahead_sum += pick(tables[j][2], row) * c + pick(tables[j][3], row) * s
        return back_sum, ahead_sum

    def target(k):
        step = jnp.where(lax.rem(k, 2) == 0, k // 2, ring - (k + 1) // 2)
        return lax.rem(chip + ring // 2 + step, ring)

    def partial_step(k, carry):
        first = target(k) * 2 * share
        for t in range(tiles):
            base = pl.multiple_of(first + (1 - core) * share + t * SUB, SUB)
            theirs[k, 0, pl.ds(t * SUB, SUB), :], theirs[k, 1, pl.ds(t * SUB, SUB), :] = partial(base)
        for t in range(tiles):
            base = pl.multiple_of(first + core * share + t * SUB, SUB)
            mine[k, 0, pl.ds(t * SUB, SUB), :], mine[k, 1, pl.ds(t * SUB, SUB), :] = partial(base)
        return carry

    lax.fori_loop(0, ring, partial_step, 0)
    for t in range(tiles):
        at = pl.ds(t * SUB, SUB)
        row = rows[pl.ds(pl.multiple_of(harm * share + t * SUB, SUB), SUB), :]
        value = gathered[harm, at, :]
        mine[ring - 1, 0, at, :] += pick(back_gain, row) * value
        mine[ring - 1, 1, at, :] += pick(ahead_gain, row) * value

    pl.semaphore_wait(barrier, 3 * ring)

    def remote(src, dst, send, recv, device):
        return pltpu.make_async_remote_copy(
            src_ref=src, dst_ref=dst, send_sem=send, recv_sem=recv, device_id=device, device_id_type=MESH
        )

    pair = [
        remote(theirs.at[k], inbox.at[k], pair_send.at[k], pair_recv.at[k], (blk, partner))
        for k in range(ring)
    ]
    around = [
        remote(gathered.at[harm], gathered.at[harm], ring_send.at[k], ring_recv.at[k], (blk, peer(hops[k])))
        for k in range(ring - 1)
    ]
    sums = [
        [
            remote(outbox.at[k, i], arrived.at[k, i], sum_send.at[k, i], sum_recv.at[k, i], (b, peer(hops[k])))
            for i, b in enumerate((after, before))
        ]
        for k in range(ring)
    ]
    forward = []
    for k in range(ring):
        source = gathered.at[peer(ring - hops[k])]
        forward.append(remote(source, source, fwd_send.at[k], fwd_recv.at[k], (blk, partner)))

    pair[0].start()
    pair[1].start()
    for k in range(ring - 1):
        around[k].start()
    for k in range(2, ring):
        pair[k].start()
    forward[ring - 1].start()
    for k in range(ring):
        pair[k].wait_recv()
        outbox[k] = mine[k] + inbox[k]
        if k:
            for copy in sums[k - 1]:
                copy.start()

    for k in range(ring - 2, -1, -1):
        around[k].wait_recv()
        forward[k].start()
        if k == ring - 2:
            for copy in sums[ring - 1]:
                copy.start()
    for k in range(ring - 1, -1, -1):
        forward[k].wait_recv()

    def update_step(i, carry):
        for t in range(tiles):
            at = pl.ds(pl.multiple_of(i * share + t * SUB, SUB), SUB)
            row = rows[at, :]
            value = gathered[i, pl.ds(t * SUB, SUB), :]
            for j in range(slots):
                hold = pick(coef[j, 6], row)
                new_store[0, j, at, :] = hold * store[0, j, at, :] + pick(coef[j, 4], row) * value
                new_store[1, j, at, :] = hold * store[1, j, at, :] + pick(coef[j, 5], row) * value
        return carry

    lax.fori_loop(0, n_harm, update_step, 0)

    for i, out in enumerate((lower, upper)):
        total = None
        for k in range(ring - 1, -1, -1):
            sums[k][i].wait_recv()
            total = arrived[k, i] if total is None else total + arrived[k, i]
        out[...] = total
    for k in range(ring):
        pair[k].wait_send()
        forward[k].wait_send()
        if k < ring - 1:
            around[k].wait_send()
        for copy in sums[k]:
            copy.wait_send()


def write_kernel(a, b, c, a_out, b_out, c_out, sems):
    copies = [
        pltpu.make_async_copy(src, dst, sems.at[i])
        for i, (src, dst) in enumerate(((a, a_out), (b, b_out), (c, c_out)))
    ]
    for copy in copies:
        copy.start()
    for copy in copies:
        copy.wait()


def solution(mesh):
    n_blk, n_harm = mesh.shape["blk"], mesh.shape["harm"]
    ring = n_harm // 2

    def shards(samples, store, phase, patch_row, harm_counts, freq_index, blade_counts):
        share, points = samples.shape
        _, slots, patches, _ = store.shape
        f32 = jnp.float32
        any_spec = pl.BlockSpec(memory_space=pl.ANY)
        smem = pl.BlockSpec(memory_space=pltpu.SMEM)
        vmem = pl.BlockSpec(memory_space=pltpu.VMEM)
        dma = pltpu.SemaphoreType.DMA
        outs = (
            pltpu.VMEM(store.shape, f32),
            pltpu.VMEM(samples.shape, f32),
            pltpu.VMEM(samples.shape, f32),
        )
        block = (ring, 2, share, points)
        results = pl.pallas_call(
            functools.partial(fourier_kernel, n_blk, n_harm),
            name="fourier",
            out_shape=outs,
            in_specs=[any_spec, any_spec, smem, vmem, smem, vmem, smem],
            out_specs=[vmem, vmem, vmem],
            scratch_shapes=[
                pltpu.VMEM(store.shape, f32),
                pltpu.VMEM((n_harm, share, points), f32),
                pltpu.VMEM((SUB, LANES), f32),
                pltpu.VMEM((patches, LANES), jnp.int32),
                pltpu.VMEM((slots, 7, SUB, LANES), f32),
                pltpu.VMEM(block, f32),
                pltpu.VMEM(block, f32),
                pltpu.VMEM(block, f32),
                pltpu.VMEM(block, f32),
                pltpu.VMEM(block, f32),
                dma((2 * slots + 1,)),
                dma((ring,)),
                dma((ring,)),
                dma((ring, 2)),
                dma((ring, 2)),
                dma((ring - 1,)),
                dma((ring - 1,)),
                dma((ring,)),
                dma((ring,)),
            ],
            compiler_params=pltpu.CompilerParams(collective_id=0, has_side_effects=True),
        )(
            samples,
            store,
            phase,
            patch_row.reshape(patches // LANES, LANES),
            harm_counts,
            freq_index,
            blade_counts,
        )
        results = [pltpu.with_memory_space_constraint(r, pltpu.VMEM) for r in results]
        return pl.pallas_call(
            write_kernel,
            name="write",
            out_shape=tuple(jax.ShapeDtypeStruct(o.shape, f32) for o in outs),
            in_specs=[vmem, vmem, vmem],
            out_specs=[any_spec, any_spec, any_spec],
            scratch_shapes=[dma((3,))],
        )(*results)

    in_specs = (P(("blk", "harm"), None), P(None, "harm", "blk", None), P(), P("blk"), P(), P(), P())
    out_specs = (P(None, "harm", "blk", None), P(("blk", "harm"), None), P(("blk", "harm"), None))
    return jax.shard_map(shards, mesh=mesh, in_specs=in_specs, out_specs=out_specs, check_vma=False)
```

time: 119 us -> 29.4 us (0.25)
  waiting for transfers between devices: 58.7 us -> 0 us
  Pallas kernels: 0 us -> 28.6 us
  blocking collectives: 25.4 us -> 0 us
  between operations: 14.1 us -> 0.64 us
  other arithmetic: 9.56 us -> 0 us
  starting transfers between devices: 8.34 us -> 0 us
  local copies, waits for them, and re-layouts: 1.95 us -> 0 us
    reduce_scatter x1 -> x0, waiting for transfers between devices: 54 us -> none  [shards(): lax.psum_scatter(jnp.stack([back_part, ahead_part]), 'harm', scatter_dime...]
    pallas_call x0 -> x2, Pallas kernels: none -> 28.6 us  [the longest x1 27.4 us: shards(): pl.pallas_call(functools.partial(fourier_kernel, n_blk, n_harm), name='fo...]
    all_gather x1 -> x0, blocking collectives: 25.4 us -> none  [shards(): gathered = lax.all_gather(samples, 'harm', axis=0, tiled=True)]
    ppermute x2 -> x0, starting transfers between devices: 8.3 us -> none  [from_behind(): return lax.ppermute(block, axis, route)]
    ppermute x2 -> x0, waiting for transfers between devices: 4.63 us -> none  [from_behind(): return lax.ppermute(block, axis, route)]
    reduce_sum x2 -> x0, other arithmetic: 3.66 us -> none  [the longest x1 3.56 us: shards(): jnp.sum(jnp.where(active_mask, cos_new * jnp.cos(back_angle) + sin_new *...]
    another operation x2 -> x0, other arithmetic: 2.07 us -> none  [the longest x1 1.25 us: shards(): new_store = jnp.stack([cos_new, sin_new])]
    convert_element_type x2 -> x0, other arithmetic: 1.38 us -> none  [the longest x1 0.72 us: shards(): active_row = (slot_ids[None, :] < harm_counts[:, None]).astype(jnp.float32)]
  transfers between devices with their start and end apart: 3 -> 0, of which waited for: 2 -> 0; matrix products, arithmetic and copies ran while one was open for 2% -> 0% of each run, Pallas kernels for 0% -> 0%
where the time goes in v1:
time: 29.4 us; the launch traced here: 29.2 us
  Pallas kernels  28.6 us (97%)
  between operations  0.64 us (2%)
    pallas_call x1, Pallas kernels, shards(): pl.pallas_call(functools.partial(fourier_kernel, n_blk, n_harm), name='fo...  27.4 us
    pallas_call x1, Pallas kernels, shards(): pl.pallas_call(write_kernel, name='write', out_shape=tuple((jax.ShapeDtyp...  1.18 us

profile of v1, /device:TPU:1, one launch (start us, length us, event | category | flops | bytes accessed | tf_op | source)
XLA Modules:
  0.0 29.2 jit_solution(8979006245876767301)
XLA Ops:
  0.6 27.4 %fourier.1 = (f32[2,3,512,128]{3,2,1,0:T(8,128)S(1)}, f32[32,128]{1,0:T(8,128)S(1)}, f32[32,128]{1,0:T(8,128)S(1)}) custom-call(f32[32,128]{1,0:T(8,128)} %samples_hbm.1, f32[2,3,512,128]{3,2,1,0:T(8,128)} %store_hbm.1, f32[5]{0:T(128)} %phase.1, s32[4,128]{1,0:T(4,128)} %bitcast.1, s32[5]{0:T(128)} %harm_counts.1, s32[5,48]{1,0:T(8,128)} %freq_index.1, ...), custom_call_target="tpu_custom_call" | custom-call | tf_op jit(solution)/shard_map/fourier/pallas_call | solution.py:280
  28.1 1.2 %write.1 = (f32[2,3,512,128]{3,2,1,0:T(8,128)}, f32[32,128]{1,0:T(8,128)}, f32[32,128]{1,0:T(8,128)}) custom-call(f32[2,3,512,128]{3,2,1,0:T(8,128)S(1)} %get-tuple-element.6.a, f32[32,128]{1,0:T(8,128)S(1)} %get-tuple-element.7.b, f32[32,128]{1,0:T(8,128)S(1)} %get-tuple-element.8.c), custom_call_target="tpu_custom_call" | custom-call | tf_op jit(solution)/shard_map/write/pallas_call | solution.py:318

commit v2 on v1

v2 whole, which is shorter than its diff:
```python
import functools

import jax
import jax.numpy as jnp
from jax import lax
from jax.experimental import pallas as pl
from jax.experimental.pallas import tpu as pltpu
from jax.sharding import PartitionSpec as P

MESH = pl.DeviceIdType.MESH
relax_rate = 0.3
LANES = 128
SUB = 8


HOPS = (3, 5, 4, 2, 6, 1, 7, 0)


def fourier_kernel(
    n_blk,
    n_harm,
    samples_hbm,
    store_hbm,
    phase_hbm,
    patch_row_hbm,
    harm_counts_hbm,
    freq_index_hbm,
    blade_counts_hbm,
    new_store,
    lower,
    upper,
    store,
    gathered,
    freq,
    rows,
    coef,
    mine,
    theirs,
    inbox,
    outbox,
    passing,
    arrived,
    phase,
    harm_counts,
    blade_counts,
    patch_row,
    freq_index,
    beyond,
    small_sem,
    own_sem,
    load_sem,
    pair_send,
    pair_recv,
    pass_send,
    pass_recv,
    sum_send,
    sum_recv,
    ring_send,
    ring_recv,
    fwd_send,
    fwd_recv,
):
    slots, patches = store.shape[1], store.shape[2]
    row_count, slot_total = freq_index.shape
    ring = n_harm // 2
    share = patches // n_harm
    tiles = share // SUB
    blk = lax.axis_index("blk")
    harm = lax.axis_index("harm")
    chip, core = harm // 2, harm % 2
    partner = 2 * chip + 1 - core
    after = lax.rem(blk + 1, n_blk)
    before = lax.rem(blk + n_blk - 1, n_blk)

    def signal(sem, b, h):
        pl.semaphore_signal(sem, 1, device_id=(b, h), device_id_type=MESH)

    def remote(src, dst, send, recv, device):
        return pltpu.make_async_remote_copy(
            src_ref=src, dst_ref=dst, send_sem=send, recv_sem=recv, device_id=device, device_id_type=MESH
        )

    def peer(d):
        return 2 * lax.rem(chip + d, ring) + core

    def peer(d):
        return 2 * lax.rem(chip + d, ring) + core

    barrier = pltpu.get_barrier_semaphore()
    for d in (2, 6, 1, 7):
        signal(barrier, blk, peer(d))
    for b, h in ((after, harm), (before, harm), (blk, partner)):
        signal(barrier, b, h)

    small = []
    for i, (src, dst) in enumerate(
        (
            (phase_hbm, phase),
            (harm_counts_hbm, harm_counts),
            (blade_counts_hbm, blade_counts),
            (freq_index_hbm, freq_index),
            (patch_row_hbm, patch_row),
        )
    ):
        small.append(pltpu.make_async_copy(src, dst, small_sem.at[i]))
        small[-1].start()

    def chip_at(k):
        return lax.rem(chip + HOPS[k], ring)

    loads = []
    for k in range(ring):
        at = pl.ds(pl.multiple_of(chip_at(k) * 2 * share, 2 * share), 2 * share)
        loads.append(pltpu.make_async_copy(store_hbm.at[:, :, at], store.at[:, :, at], load_sem.at[k]))
        loads[-1].start()
    own = pltpu.make_async_copy(samples_hbm, gathered.at[harm], own_sem)
    own.start()

    for copy in small:
        copy.wait()
    sub = lax.broadcasted_iota(jnp.int32, (SUB, LANES), 0)
    lane = lax.broadcasted_iota(jnp.int32, (SUB, LANES), 1)
    freq[...] = jnp.zeros((SUB, LANES), jnp.float32)
    freq[:row_count, :slot_total] = freq_index[...].astype(jnp.float32)
    frequency = freq[...]

    def by_row(ref, other):
        out = jnp.full((SUB, LANES), other)
        for r in range(row_count):
            out = jnp.where(sub == r, ref[r], out)
        return out

    now = frequency * by_row(phase, jnp.float32(0))
    blades = by_row(blade_counts, jnp.int32(1)).astype(jnp.float32)
    lag = 2.0 * jnp.pi * frequency / blades
    active = lane < by_row(harm_counts, jnp.int32(0))
    now_cos, now_sin = jnp.cos(now), jnp.sin(now)
    back, ahead = now - lag, now + lag
    back_cos, back_sin = jnp.cos(back), jnp.sin(back)
    ahead_cos, ahead_sin = jnp.cos(ahead), jnp.sin(ahead)
    gain = 2.0 * relax_rate
    keep = 1.0 - relax_rate
    zero = jnp.zeros((SUB, LANES), jnp.float32)

    def spread(table):
        return jnp.broadcast_to(jnp.sum(table, axis=1, keepdims=True), (SUB, LANES))

    for j in range(slots):
        here = lane == harm * slots + j
        on = active & here
        for i, table in enumerate((back_cos, back_sin, ahead_cos, ahead_sin)):
            coef[j, i] = spread(jnp.where(on, keep * table, zero))
        coef[j, 4] = spread(jnp.where(on, gain * now_cos, zero))
        coef[j, 5] = spread(jnp.where(on, gain * now_sin, zero))
        coef[j, 6] = spread(jnp.where(here, jnp.where(active, keep, 1.0), zero))
    back_gain = spread(jnp.where(active, gain * (now_cos * back_cos + now_sin * back_sin), zero))
    ahead_gain = spread(jnp.where(active, gain * (now_cos * ahead_cos + now_sin * ahead_sin), zero))

    for i in range(patches // LANES):
        line = jnp.broadcast_to(patch_row[i : i + 1, :], (LANES, LANES))
        rows[pl.ds(i * LANES, LANES), :] = line.T

    def pick(table, row):
        return jnp.take_along_axis(table, row, axis=0, mode="promise_in_bounds")

    tables = [[coef[j, i] for i in range(4)] for j in range(slots)]

    def partial(base):
        row = rows[pl.ds(base, SUB), :]
        back_sum, ahead_sum = zero, zero
        for j in range(slots):
            c, s = store[0, j, pl.ds(base, SUB), :], store[1, j, pl.ds(base, SUB), :]
            back_sum += pick(tables[j][0], row) * c + pick(tables[j][1], row) * s
            ahead_sum += pick(tables[j][2], row) * c + pick(tables[j][3], row) * s
        return back_sum, ahead_sum

    def step_chip(k):
        d = jnp.where(k < 2, 3 + 2 * k, jnp.where(k == 2, 4, jnp.where(k == 7, 0, 0)))
        d = jnp.where(k == 3, 2, jnp.where(k == 4, 6, jnp.where(k == 5, 1, jnp.where(k == 6, 7, d))))
        return lax.rem(chip + d, ring)

    def pair_copy(k):
        return remote(theirs.at[k], inbox.at[k], pair_send, pair_recv.at[k], (blk, partner))

    def partial_step(k, carry):
        at = pl.ds(pl.multiple_of(step_chip(k) * 2 * share, 2 * share), 2 * share)
        pltpu.make_async_copy(store_hbm.at[:, :, at], store.at[:, :, at], load_sem.at[k]).wait()
        first = step_chip(k) * 2 * share
        for t in range(tiles):
            base = pl.multiple_of(first + (1 - core) * share + t * SUB, SUB)
            theirs[k, 0, pl.ds(t * SUB, SUB), :], theirs[k, 1, pl.ds(t * SUB, SUB), :] = partial(base)
        for t in range(tiles):
            base = pl.multiple_of(first + core * share + t * SUB, SUB)
            mine[k, 0, pl.ds(t * SUB, SUB), :], mine[k, 1, pl.ds(t * SUB, SUB), :] = partial(base)
        return carry

    lax.fori_loop(0, ring, partial_step, 0)
    own.wait()

    def update(h):
        for t in range(tiles):
            at = pl.ds(pl.multiple_of(h * share + t * SUB, SUB), SUB)
            row = rows[at, :]
            value = gathered[h, pl.ds(t * SUB, SUB), :]
            for j in range(slots):
                hold = pick(coef[j, 6], row)
                new_store[0, j, at, :] = hold * store[0, j, at, :] + pick(coef[j, 4], row) * value
                new_store[1, j, at, :] = hold * store[1, j, at, :] + pick(coef[j, 5], row) * value

    pl.semaphore_wait(barrier, 7)
    signal(beyond, after, harm)
    signal(beyond, before, harm)

    def place(d):
        return gathered.at[peer(d)]

    def block_to(d, recv):
        return remote(samples_hbm, place(0), ring_send, ring_recv.at[recv], (blk, peer(d)))

    def forward(slot, d):
        return remote(place(d) if d else samples_hbm, place(d), fwd_send, fwd_recv.at[slot], (blk, partner))

    for k in range(3):
        pair_copy(k).start()
    block_to(2, 2).start()
    block_to(6, 3).start()
    for k in range(3, ring):
        pair_copy(k).start()
    forward(0, 0).start()

    def sums_to(k):
        for i, b in enumerate((after, before)):
            source, target = outbox.at[k, i], arrived.at[k - 3, i]
            remote(source, target, sum_send, sum_recv, (b, peer(HOPS[k]))).start()

    def far(k):
        if k < 2:
            at = pl.ds(2 * k, 2)
            sem = pass_recv.at[k]
            remote(outbox.at[k], passing.at[at], pass_send, sem, (blk, peer((1, 7)[k]))).start()
        else:
            pass_back.start()
            pass_ahead.start()

    pass_back = remote(outbox.at[2, 0], passing.at[4], pass_send, pass_recv.at[2], (blk, peer(2)))
    pass_ahead = remote(outbox.at[2, 1], passing.at[5], pass_send, pass_recv.at[3], (blk, peer(6)))

    update(harm)
    for k in range(ring - 1):
        pair_copy(k).wait_recv()
        outbox[k] = mine[k] + inbox[k]
        if 1 <= k <= 3:
            far(k - 1)
        if k == 3:
            block_to(1, 0).start()
            block_to(7, 1).start()
    pair_copy(ring - 1).wait_recv()
    for t in range(tiles):
        at = pl.ds(t * SUB, SUB)
        row = rows[pl.ds(pl.multiple_of(harm * share + t * SUB, SUB), SUB), :]
        value = gathered[harm, at, :]
        k = ring - 1
        outbox[k, 0, at, :] = mine[k, 0, at, :] + inbox[k, 0, at, :] + pick(back_gain, row) * value
        outbox[k, 1, at, :] = mine[k, 1, at, :] + inbox[k, 1, at, :] + pick(ahead_gain, row) * value

    top, bottom = pl.ds(0, share // 2), pl.ds(share // 2, share // 2)

    def relay(src, slot, d):
        return remote(src, src, ring_send, ring_recv.at[slot], (blk, peer(d)))

    block_to(2, 2).wait_recv()
    relay(place(6), 4, 1).start()
    relay(place(6).at[top], 6, 2).start()
    block_to(6, 3).wait_recv()
    relay(place(2), 5, 7).start()
    relay(place(2).at[bottom], 7, 6).start()
    forward(1, 6).start()
    forward(2, 2).start()

    pl.semaphore_wait(beyond, 2)
    for k in (5, 6, 7):
        sums_to(k)

    def received(ref, sem):
        pltpu.make_async_copy(ref, ref, sem).wait()

    received(passing.at[pl.ds(0, 2)], pass_recv.at[0])
    received(passing.at[4], pass_recv.at[2])
    outbox[3, 0] = outbox[3, 0] + passing[0] + passing[4]
    outbox[3, 1] = outbox[3, 1] + passing[1]
    received(passing.at[pl.ds(2, 2)], pass_recv.at[1])
    received(passing.at[5], pass_recv.at[3])
    outbox[4, 0] = outbox[4, 0] + passing[2]
    outbox[4, 1] = outbox[4, 1] + passing[3] + passing[5]
    sums_to(3)
    update(peer(6))
    sums_to(4)
    update(peer(2))
    block_to(1, 0).wait_recv()
    forward(3, 7).start()
    block_to(7, 1).wait_recv()
    forward(4, 1).start()
    update(peer(7))
    update(peer(1))

    received(place(5), ring_recv.at[4])
    forward(5, 5).start()
    received(place(3), ring_recv.at[5])
    forward(6, 3).start()
    received(place(4).at[top], ring_recv.at[6])
    received(place(4).at[bottom], ring_recv.at[7])
    forward(7, 4).start()
    for d in (5, 3, 4):
        update(peer(d))
    for slot, d in enumerate((0, 6, 2, 7, 1, 5, 3, 4)):
        h = 2 * lax.rem(chip + d, ring) + 1 - core
        received(gathered.at[h], fwd_recv.at[slot])
        update(h)

    received(arrived, sum_recv)
    for i, out in enumerate((lower, upper)):
        total = arrived[0, i]
        for k in range(1, arrived.shape[0]):
            total += arrived[k, i]
        out[...] = total
    received(theirs, pair_send)
    received(outbox.at[pl.ds(0, 3)], pass_send)
    received(arrived, sum_send)
    received(gathered.at[pl.ds(0, 7)], ring_send)
    received(gathered.at[pl.ds(0, ring)], fwd_send)


def write_kernel(a, b, c, a_out, b_out, c_out, sems):
    copies = [
        pltpu.make_async_copy(src, dst, sems.at[i])
        for i, (src, dst) in enumerate(((a, a_out), (b, b_out), (c, c_out)))
    ]
    for copy in copies:
        copy.start()
    for copy in copies:
        copy.wait()


def solution(mesh):
    n_blk, n_harm = mesh.shape["blk"], mesh.shape["harm"]
    ring = n_harm // 2

    def shards(samples, store, phase, patch_row, harm_counts, freq_index, blade_counts):
        share, points = samples.shape
        _, slots, patches, _ = store.shape
        f32 = jnp.float32
        any_spec = pl.BlockSpec(memory_space=pl.ANY)
        vmem = pl.BlockSpec(memory_space=pltpu.VMEM)
        dma = pltpu.SemaphoreType.DMA
        outs = (
            pltpu.VMEM(store.shape, f32),
            pltpu.VMEM(samples.shape, f32),
            pltpu.VMEM(samples.shape, f32),
        )
        block = (ring, 2, share, points)
        results = pl.pallas_call(
            functools.partial(fourier_kernel, n_blk, n_harm),
            name="fourier",
            out_shape=outs,
            in_specs=[any_spec] * 7,
            out_specs=[vmem, vmem, vmem],
            scratch_shapes=[
                pltpu.VMEM(store.shape, f32),
                pltpu.VMEM((n_harm, share, points), f32),
                pltpu.VMEM((SUB, LANES), f32),
                pltpu.VMEM((patches, LANES), jnp.int32),
                pltpu.VMEM((slots, 7, SUB, LANES), f32),
                pltpu.VMEM(block, f32),
                pltpu.VMEM(block, f32),
                pltpu.VMEM(block, f32),
                pltpu.VMEM(block, f32),
                pltpu.VMEM((6, share, points), f32),
                pltpu.VMEM((5, 2, share, points), f32),
                pltpu.SMEM(phase.shape, f32),
                pltpu.SMEM(harm_counts.shape, jnp.int32),
                pltpu.SMEM(blade_counts.shape, jnp.int32),
                pltpu.VMEM((patches // LANES, LANES), jnp.int32),
                pltpu.VMEM(freq_index.shape, jnp.int32),
                pltpu.SemaphoreType.REGULAR,
                dma((5,)),
                dma(()),
                dma((ring,)),
                dma(()),
                dma((ring,)),
                dma(()),
                dma((4,)),
                dma(()),
                dma(()),
                dma(()),
                dma((8,)),
                dma(()),
                dma((ring,)),
            ],
            compiler_params=pltpu.CompilerParams(collective_id=0, has_side_effects=True),
        )(
            samples,
            store,
            phase,
            patch_row.reshape(patches // LANES, LANES),
            harm_counts,
            freq_index,
            blade_counts,
        )
        results = [pltpu.with_memory_space_constraint(r, pltpu.VMEM) for r in results]
        return pl.pallas_call(
            write_kernel,
            name="write",
            out_shape=tuple(jax.ShapeDtypeStruct(o.shape, f32) for o in outs),
            in_specs=[vmem, vmem, vmem],
            out_specs=[any_spec, any_spec, any_spec],
            scratch_shapes=[dma((3,))],
        )(*results)

    in_specs = (P(("blk", "harm"), None), P(None, "harm", "blk", None), P(), P("blk"), P(), P(), P())
    out_specs = (P(None, "harm", "blk", None), P(("blk", "harm"), None), P(("blk", "harm"), None))
    return jax.shard_map(shards, mesh=mesh, in_specs=in_specs, out_specs=out_specs, check_vma=False)
```

time: 29.4 us -> 26.7 us (0.908)
  Pallas kernels: 28.6 us -> 25.9 us
    pallas_call x1, Pallas kernels: 27.4 us -> 24.7 us  [shards(): pl.pallas_call(functools.partial(fourier_kernel, n_blk, n_harm), name='fo...]
where the time goes in v2:
time: 26.7 us; the launch traced here: 26.5 us
  Pallas kernels  25.9 us (97%)
  between operations  0.64 us (2%)
    pallas_call x1, Pallas kernels, shards(): pl.pallas_call(functools.partial(fourier_kernel, n_blk, n_harm), name='fo...  24.7 us
    pallas_call x1, Pallas kernels, shards(): pl.pallas_call(write_kernel, name='write', out_shape=tuple((jax.ShapeDtyp...  1.18 us

profile of v2, /device:TPU:1, one launch (start us, length us, event | category | flops | bytes accessed | tf_op | source)
XLA Modules:
  0.0 26.5 jit_solution(12831566046813359733)
XLA Ops:
  0.6 24.7 %fourier.1 = (f32[2,3,512,128]{3,2,1,0:T(8,128)S(1)}, f32[32,128]{1,0:T(8,128)S(1)}, f32[32,128]{1,0:T(8,128)S(1)}) custom-call(f32[32,128]{1,0:T(8,128)} %samples_hbm.1, f32[2,3,512,128]{3,2,1,0:T(8,128)} %store_hbm.1, f32[5]{0:T(128)} %phase_hbm.1, s32[4,128]{1,0:T(4,128)} %bitcast.1, s32[5]{0:T(128)} %harm_counts_hbm.1, s32[5,48]{1,0:T(8,128)} %freq_index_hbm.1, ...), custom_call_target="tpu_custom_call" | custom-call | tf_op jit(solution)/shard_map/fourier/pallas_call | solution.py:361
  25.3 1.2 %write.1 = (f32[2,3,512,128]{3,2,1,0:T(8,128)}, f32[32,128]{1,0:T(8,128)}, f32[32,128]{1,0:T(8,128)}) custom-call(f32[2,3,512,128]{3,2,1,0:T(8,128)S(1)} %get-tuple-element.6.a, f32[32,128]{1,0:T(8,128)S(1)} %get-tuple-element.7.b, f32[32,128]{1,0:T(8,128)S(1)} %get-tuple-element.8.c), custom_call_target="tpu_custom_call" | custom-call | tf_op jit(solution)/shard_map/write/pallas_call | solution.py:410

commit v3 on v2

--- a/solution.py
+++ b/solution.py
@@ -13,7 +13,7 @@
 SUB = 8
 
 
-HOPS = (3, 5, 4, 2, 6, 1, 7, 0)
+HOPS = (4, 3, 5, 2, 6, 1, 7, 0)
 
 
 def fourier_kernel(
@@ -45,6 +45,7 @@
     blade_counts,
     patch_row,
     freq_index,
+    around,
     beyond,
     small_sem,
     own_sem,
@@ -88,9 +89,13 @@
 
     barrier = pltpu.get_barrier_semaphore()
     for d in (2, 6, 1, 7):
-        signal(barrier, blk, peer(d))
-    for b, h in ((after, harm), (before, harm), (blk, partner)):
-        signal(barrier, b, h)
+        signal(barrier, blk, peer(d) - core)
+    signal(barrier, after, 2 * chip + 1)
+    signal(barrier, before, 2 * chip + 1)
+
+    @pl.when(core == 1)
+    def _():
+        signal(barrier, blk, partner)
 
     small = []
     for i, (src, dst) in enumerate(
@@ -112,12 +117,15 @@
     for k in range(ring):
         at = pl.ds(pl.multiple_of(chip_at(k) * 2 * share, 2 * share), 2 * share)
         loads.append(pltpu.make_async_copy(store_hbm.at[:, :, at], store.at[:, :, at], load_sem.at[k]))
-        loads[-1].start()
+        if k < 3:
+            loads[-1].start()
     own = pltpu.make_async_copy(samples_hbm, gathered.at[harm], own_sem)
     own.start()
 
     for copy in small:
         copy.wait()
+    for k in range(3, ring):
+        loads[k].start()
     sub = lax.broadcasted_iota(jnp.int32, (SUB, LANES), 0)
     lane = lax.broadcasted_iota(jnp.int32, (SUB, LANES), 1)
     freq[...] = jnp.zeros((SUB, LANES), jnp.float32)
@@ -175,9 +183,8 @@
         return back_sum, ahead_sum
 
     def step_chip(k):
-        d = jnp.where(k < 2, 3 + 2 * k, jnp.where(k == 2, 4, jnp.where(k == 7, 0, 0)))
-        d = jnp.where(k == 3, 2, jnp.where(k == 4, 6, jnp.where(k == 5, 1, jnp.where(k == 6, 7, d))))
-        return lax.rem(chip + d, ring)
+        step = jnp.where(lax.rem(k, 2) == 0, k // 2, ring - (k + 1) // 2)
+        return lax.rem(chip + ring // 2 + step, ring)
 
     def pair_copy(k):
         return remote(theirs.at[k], inbox.at[k], pair_send, pair_recv.at[k], (blk, partner))
@@ -194,8 +201,7 @@
             mine[k, 0, pl.ds(t * SUB, SUB), :], mine[k, 1, pl.ds(t * SUB, SUB), :] = partial(base)
         return carry
 
-    lax.fori_loop(0, ring, partial_step, 0)
-    own.wait()
+    lax.fori_loop(0, 3, partial_step, 0)
 
     def update(h):
         for t in range(tiles):
@@ -207,9 +213,14 @@
                 new_store[0, j, at, :] = hold * store[0, j, at, :] + pick(coef[j, 4], row) * value
                 new_store[1, j, at, :] = hold * store[1, j, at, :] + pick(coef[j, 5], row) * value
 
-    pl.semaphore_wait(barrier, 7)
-    signal(beyond, after, harm)
-    signal(beyond, before, harm)
+    @pl.when(core == 0)
+    def _():
+        pl.semaphore_wait(barrier, 9)
+        signal(around, blk, partner)
+
+    @pl.when(core == 1)
+    def _():
+        pl.semaphore_wait(around, 1)
 
     def place(d):
         return gathered.at[peer(d)]
@@ -224,9 +235,8 @@
         pair_copy(k).start()
     block_to(2, 2).start()
     block_to(6, 3).start()
-    for k in range(3, ring):
-        pair_copy(k).start()
     forward(0, 0).start()
+    lax.fori_loop(3, ring, partial_step, 0)
 
     def sums_to(k):
         for i, b in enumerate((after, before)):
@@ -234,26 +244,32 @@
             remote(source, target, sum_send, sum_recv, (b, peer(HOPS[k]))).start()
 
     def far(k):
-        if k < 2:
-            at = pl.ds(2 * k, 2)
-            sem = pass_recv.at[k]
-            remote(outbox.at[k], passing.at[at], pass_send, sem, (blk, peer((1, 7)[k]))).start()
+        if k:
+            at = pl.ds(2 * k - 2, 2)
+            sem = pass_recv.at[k - 1]
+            remote(outbox.at[k], passing.at[at], pass_send, sem, (blk, peer((1, 7)[k - 1]))).start()
         else:
             pass_back.start()
             pass_ahead.start()
 
-    pass_back = remote(outbox.at[2, 0], passing.at[4], pass_send, pass_recv.at[2], (blk, peer(2)))
-    pass_ahead = remote(outbox.at[2, 1], passing.at[5], pass_send, pass_recv.at[3], (blk, peer(6)))
-
-    update(harm)
-    for k in range(ring - 1):
+    pass_back = remote(outbox.at[0, 0], passing.at[4], pass_send, pass_recv.at[2], (blk, peer(2)))
+    pass_ahead = remote(outbox.at[0, 1], passing.at[5], pass_send, pass_recv.at[3], (blk, peer(6)))
+
+    for k in range(3):
         pair_copy(k).wait_recv()
         outbox[k] = mine[k] + inbox[k]
-        if 1 <= k <= 3:
+        if k:
             far(k - 1)
-        if k == 3:
-            block_to(1, 0).start()
-            block_to(7, 1).start()
+    for k in range(3, ring):
+        pair_copy(k).start()
+    far(2)
+    block_to(1, 0).start()
+    block_to(7, 1).start()
+    own.wait()
+    update(harm)
+    for k in range(3, ring - 1):
+        pair_copy(k).wait_recv()
+        outbox[k] = mine[k] + inbox[k]
     pair_copy(ring - 1).wait_recv()
     for t in range(tiles):
         at = pl.ds(t * SUB, SUB)
@@ -262,6 +278,13 @@
         k = ring - 1
         outbox[k, 0, at, :] = mine[k, 0, at, :] + inbox[k, 0, at, :] + pick(back_gain, row) * value
         outbox[k, 1, at, :] = mine[k, 1, at, :] + inbox[k, 1, at, :] + pick(ahead_gain, row) * value
+
+    @pl.when(core == 1)
+    def _():
+        pl.semaphore_wait(barrier, 4)
+        for b in (after, before):
+            signal(beyond, b, 2 * chip)
+            signal(beyond, b, 2 * chip + 1)
 
     top, bottom = pl.ds(0, share // 2), pl.ds(share // 2, share // 2)
 
@@ -382,6 +405,7 @@
                 pltpu.VMEM((patches // LANES, LANES), jnp.int32),
                 pltpu.VMEM(freq_index.shape, jnp.int32),
                 pltpu.SemaphoreType.REGULAR,
+                pltpu.SemaphoreType.REGULAR,
                 dma((5,)),
                 dma(()),
                 dma((ring,)),

time: 26.7 us -> 25.7 us (0.963)
  Pallas kernels: 25.9 us -> 24.9 us
    pallas_call x1, Pallas kernels: 24.7 us -> 23.8 us  [shards(): pl.pallas_call(functools.partial(fourier_kernel, n_blk, n_harm), name='fo...]
where the time goes in v3:
time: 25.7 us; the launch traced here: 25.6 us
  Pallas kernels  24.9 us (97%)
  between operations  0.64 us (2%)
    pallas_call x1, Pallas kernels, shards(): pl.pallas_call(functools.partial(fourier_kernel, n_blk, n_harm), name='fo...  23.8 us
    pallas_call x1, Pallas kernels, shards(): pl.pallas_call(write_kernel, name='write', out_shape=tuple((jax.ShapeDtyp...  1.18 us

profile of v3, /device:TPU:1, one launch (start us, length us, event | category | flops | bytes accessed | tf_op | source)
XLA Modules:
  0.0 25.6 jit_solution(9606864192744003376)
XLA Ops:
  0.6 23.8 %fourier.1 = (f32[2,3,512,128]{3,2,1,0:T(8,128)S(1)}, f32[32,128]{1,0:T(8,128)S(1)}, f32[32,128]{1,0:T(8,128)S(1)}) custom-call(f32[32,128]{1,0:T(8,128)} %samples_hbm.1, f32[2,3,512,128]{3,2,1,0:T(8,128)} %store_hbm.1, f32[5]{0:T(128)} %phase_hbm.1, s32[4,128]{1,0:T(4,128)} %bitcast.1, s32[5]{0:T(128)} %harm_counts_hbm.1, s32[5,48]{1,0:T(8,128)} %freq_index_hbm.1, ...), custom_call_target="tpu_custom_call" | custom-call | tf_op jit(solution)/shard_map/fourier/pallas_call | solution.py:384
  24.4 1.2 %write.1 = (f32[2,3,512,128]{3,2,1,0:T(8,128)}, f32[32,128]{1,0:T(8,128)}, f32[32,128]{1,0:T(8,128)}) custom-call(f32[2,3,512,128]{3,2,1,0:T(8,128)S(1)} %get-tuple-element.6.a, f32[32,128]{1,0:T(8,128)S(1)} %get-tuple-element.7.b, f32[32,128]{1,0:T(8,128)S(1)} %get-tuple-element.8.c), custom_call_target="tpu_custom_call" | custom-call | tf_op jit(solution)/shard_map/write/pallas_call | solution.py:434

commit v4 on v3

--- a/solution.py
+++ b/solution.py
@@ -237,6 +237,10 @@
     block_to(6, 3).start()
     forward(0, 0).start()
     lax.fori_loop(3, ring, partial_step, 0)
+    own.wait()
+    update(harm)
+    for k in range(3, ring):
+        pair_copy(k).start()
 
     def sums_to(k):
         for i, b in enumerate((after, before)):
@@ -260,13 +264,9 @@
         outbox[k] = mine[k] + inbox[k]
         if k:
             far(k - 1)
-    for k in range(3, ring):
-        pair_copy(k).start()
-    far(2)
     block_to(1, 0).start()
     block_to(7, 1).start()
-    own.wait()
-    update(harm)
+    far(2)
     for k in range(3, ring - 1):
         pair_copy(k).wait_recv()
         outbox[k] = mine[k] + inbox[k]

time: 25.7 us -> 26 us (1.012); the launches traced: 25.6 us -> 25.6 us
  no operation moved by 1% of the time
where the time goes in v4:
time: 26 us; the launch traced here: 25.6 us
  Pallas kernels  24.9 us (96%)
  between operations  0.64 us (2%)
    pallas_call x1, Pallas kernels, shards(): pl.pallas_call(functools.partial(fourier_kernel, n_blk, n_harm), name='fo...  23.7 us
    pallas_call x1, Pallas kernels, shards(): pl.pallas_call(write_kernel, name='write', out_shape=tuple((jax.ShapeDtyp...  1.18 us

profile of v4, /device:TPU:1, one launch (start us, length us, event | category | flops | bytes accessed | tf_op | source)
XLA Modules:
  0.0 25.6 jit_solution(206615620428891994)
XLA Ops:
  0.6 23.7 %fourier.1 = (f32[2,3,512,128]{3,2,1,0:T(8,128)S(1)}, f32[32,128]{1,0:T(8,128)S(1)}, f32[32,128]{1,0:T(8,128)S(1)}) custom-call(f32[32,128]{1,0:T(8,128)} %samples_hbm.1, f32[2,3,512,128]{3,2,1,0:T(8,128)} %store_hbm.1, f32[5]{0:T(128)} %phase_hbm.1, s32[4,128]{1,0:T(4,128)} %bitcast.1, s32[5]{0:T(128)} %harm_counts_hbm.1, s32[5,48]{1,0:T(8,128)} %freq_index_hbm.1, ...), custom_call_target="tpu_custom_call" | custom-call | tf_op jit(solution)/shard_map/fourier/pallas_call | solution.py:384
  24.4 1.2 %write.1 = (f32[2,3,512,128]{3,2,1,0:T(8,128)}, f32[32,128]{1,0:T(8,128)}, f32[32,128]{1,0:T(8,128)}) custom-call(f32[2,3,512,128]{3,2,1,0:T(8,128)S(1)} %get-tuple-element.6.a, f32[32,128]{1,0:T(8,128)S(1)} %get-tuple-element.7.b, f32[32,128]{1,0:T(8,128)S(1)} %get-tuple-element.8.c), custom_call_target="tpu_custom_call" | custom-call | tf_op jit(solution)/shard_map/write/pallas_call | solution.py:434
